TPU v7x, 32 devices: a whole 2x2x4 slice. The times are simulated.
32 devices in a mesh: rows: 8 (over z, y), mp: 4 (over x, core).
Axes of the slice: x: 2, y: 2, z: 4, core: 2. Of those that a mesh axis runs over, the one named last changes fastest.
Arguments:
- calib: bfloat16 [512, 8192], P('rows', 'mp'), may hold values from -40 to 40
- weight: bfloat16 [8192, 8192], P('rows', 'mp'), may hold values from -6 to 6
- inverse_factor: float32 [8192, 8192], P('rows', 'mp'), may hold values from -10 to 12, as said below
- pruned_blocks: int32 [7], replicated, may hold values from 0 to 63, as said below
Outputs:
- pruned_weight: bfloat16 [8192, 8192], P('rows', 'mp')
- next_gram: float32 [8192, 8192], P('rows', 'mp')
Inputs may be any that keep to these rules, and one draw needn't show every extreme that they name: `pruned_blocks`: 7 distinct block numbers in any order; block b holds rows b * 128 to b * 128 + 127. `inverse_factor`: symmetric and positive definite.
All inputs are finite; a program needn't handle non-finite values.
Results may differ from a plain program's by a relative error of at most 0.0095.
Values may be sent and summed in bfloat16 or wider, within the bound.
A program may use at most 128 MiB of HBM per device.

v0:
```python
import jax
import jax.numpy as jnp
from jax import lax
from jax.sharding import PartitionSpec as P

BLOCK = 128


def spd_solve(chol_lower, right_side):
    forward = lax.linalg.triangular_solve(chol_lower, right_side, left_side=True, lower=True)
    return lax.linalg.triangular_solve(
        chol_lower, forward, left_side=True, lower=True, transpose_a=True
    )


def shards(calib, weight, inverse_factor, pruned_blocks):
    rows_dev = weight.shape[0]
    width_dev = weight.shape[1]
    full_width = width_dev * lax.axis_size("mp")
    row_start = lax.axis_index("rows") * rows_dev
    col_start = lax.axis_index("mp") * width_dev
    starts = pruned_blocks * BLOCK
    block_count = pruned_blocks.shape[0]
    col_pieces = []
    for slot_index in range(block_count):
        offset = starts[slot_index] - col_start
        inside = ((offset >= 0) & (offset < width_dev)).astype(jnp.float32)
        clamped = jnp.clip(offset, 0, width_dev - BLOCK)
        col_pieces.append(lax.dynamic_slice_in_dim(inverse_factor, clamped, BLOCK, 1) * inside)
    columns = lax.psum(jnp.concatenate(col_pieces, axis=1), "mp")
    weight_parts = []
    inverse_parts = []
    for slot_index in range(block_count):
        offset = starts[slot_index] - row_start
        inside = ((offset >= 0) & (offset < rows_dev)).astype(jnp.float32)
        clamped = jnp.clip(offset, 0, rows_dev - BLOCK)
        weight_parts.append(
            lax.dynamic_slice_in_dim(weight, clamped, BLOCK, 0).astype(jnp.float32) * inside
        )
        inverse_parts.append(lax.dynamic_slice_in_dim(columns, clamped, BLOCK, 0) * inside)
    kept_rows = lax.psum(jnp.concatenate(weight_parts, axis=0).astype(jnp.bfloat16), "rows").astype(
        jnp.float32
    )
    inverse_square = lax.psum(jnp.concatenate(inverse_parts, axis=0), "rows")
    chol_lower = jnp.linalg.cholesky(inverse_square)
    factors = spd_solve(chol_lower, columns.T)
    update = lax.dot_general(
        factors, kept_rows, (((0,), (0,)), ((), ())), precision=lax.Precision.HIGHEST
    )
    block_ids = (row_start + jnp.arange(rows_dev, dtype=jnp.int32)) // BLOCK
    kept_mask = 1.0 - jnp.any(block_ids[:, None] == pruned_blocks[None, :], axis=1).astype(
        jnp.float32
    )
    pruned_weight = ((weight.astype(jnp.float32) - update) * kept_mask[:, None]).astype(
        jnp.bfloat16
    )
    out_scale = float(full_width) ** (-0.5)
    partial_value = lax.dot_general(
        lax.all_gather(calib, "rows", axis=0, tiled=True),
        pruned_weight,
        (((1,), (1,)), ((), ())),
        preferred_element_type=jnp.float32,
    )
    token_count = partial_value.shape[0]
    own_rows = (
        lax.psum_scatter(partial_value, "mp", scatter_dimension=0, tiled=True) * out_scale
    ).astype(jnp.bfloat16)
    gram_term = lax.dot_general(
        own_rows,
        lax.all_gather(own_rows, "rows", axis=1, tiled=True),
        (((0,), (0,)), ((), ())),
        preferred_element_type=jnp.float32,
    )
    gram_block = (
        lax.psum_scatter(
            gram_term.astype(jnp.bfloat16), "mp", scatter_dimension=1, tiled=True
        ).astype(jnp.float32)
        / token_count
    )
    return (pruned_weight, gram_block)


def solution(mesh):
    return jax.shard_map(
        shards,
        mesh=mesh,
        in_specs=(P("rows", "mp"), P("rows", "mp"), P("rows", "mp"), P()),
        out_specs=(P("rows", "mp"), P("rows", "mp")),
        check_vma=False,
    )
```

profile of v0, /device:TPU:0, one launch (start us, length us, event | category | flops | bytes accessed | tf_op | source)
XLA Modules:
  0.0 823.3 jit_solution(16125952968231039749)
XLA Ops:
  13.0 4.4 constant_dynamic-slice_fusion.1
  17.4 2.0 copy.22
  35.9 75.6 %all-reduce.5.cloned.1.call-done = f32[1024,896]{0,1:T(8,128)} async-done(((f32[1024,896]{0,1:T(8,128)}), f32[1024,896]{0,1:T(8,128)}) %all-reduce.5.cloned.1.call-update) | async-done | bytes 3670032 | tf_op jit(solution)/shard_map/psum | solution.py:30
  122.3 2.0 fusion.51
  124.3 2.0 fusion.52
  126.3 2.0 fusion.53
  128.3 2.1 fusion.54
  130.3 2.0 fusion.55
  132.3 2.0 fusion.56
  134.4 2.0 fusion.57
  137.1 116.7 %all-reduce.7.cloned.1.call-done = f32[896,896]{0,1:T(8,128)} async-done(((f32[896,896]{0,1:T(8,128)}), f32[896,896]{0,1:T(8,128)}) %all-reduce.7.cloned.1.call-update) | async-done | bytes 3211280 | tf_op jit(solution)/shard_map/psum | solution.py:44
  253.8 4.7 copy.21
  258.5 2.2 fusion
  262.5 11.7 %cholesky.195 = f32[128,128]{1,0:T(8,128)S(1)} custom-call(f32[128,128]{1,0:T(8,128)S(1)} %cholesky.502), custom_call_target="Cholesky" | custom-call | tf_op jit(solution)/shard_map/jit(cholesky)/cholesky | solution.py:45
  274.4 9.8 %custom-call.56 = f32[1,128,128]{1,2,0:T(8,128)S(1)} custom-call(f32[1,128,128]{2,1,0:T(8,128)S(1)} %get-tuple-element.55), custom_call_target="InvertDiagBlocksLowerTriangular" | custom-call | tf_op jit(solution)/shard_map/jit(cholesky)/cholesky | solution.py:45
  287.9 11.7 %cholesky.216 = f32[128,128]{1,0:T(8,128)S(1)} custom-call(f32[128,128]{1,0:T(8,128)S(1)} %cholesky.506), custom_call_target="Cholesky" | custom-call | tf_op jit(solution)/shard_map/jit(cholesky)/cholesky | solution.py:45
  301.1 10.2 %custom-call.57 = f32[1,128,128]{1,2,0:T(8,128)S(1)} custom-call(f32[1,128,128]{2,1,0:T(8,128)S(1)} %get-tuple-element.52), custom_call_target="InvertDiagBlocksLowerTriangular" | custom-call | tf_op jit(solution)/shard_map/jit(cholesky)/cholesky | solution.py:45
  314.9 13.2 %cholesky.411 = f32[128,128]{1,0:T(8,128)} custom-call(f32[128,128]{1,0:T(8,128)} %cholesky.511), custom_call_target="Cholesky" | custom-call | tf_op jit(solution)/shard_map/jit(cholesky)/cholesky | solution.py:45
  330.3 11.3 %custom-call.58 = f32[1,128,128]{1,2,0:T(8,128)} custom-call(f32[1,128,128]{2,1,0:T(8,128)} %get-tuple-element.49), custom_call_target="InvertDiagBlocksLowerTriangular" | custom-call | tf_op jit(solution)/shard_map/jit(cholesky)/cholesky | solution.py:45
  344.5 12.5 %cholesky.430 = f32[128,128]{1,0:T(8,128)} custom-call(f32[128,128]{1,0:T(8,128)S(1)} %cholesky.516), custom_call_target="Cholesky" | custom-call | tf_op jit(solution)/shard_map/jit(cholesky)/cholesky | solution.py:45
  358.6 10.4 %custom-call.59 = f32[1,128,128]{1,2,0:T(8,128)} custom-call(f32[1,128,128]{2,1,0:T(8,128)S(1)} %get-tuple-element.46), custom_call_target="InvertDiagBlocksLowerTriangular" | custom-call | tf_op jit(solution)/shard_map/jit(cholesky)/cholesky | solution.py:45
  371.9 11.7 %cholesky.449 = f32[128,128]{1,0:T(8,128)S(1)} custom-call(f32[128,128]{1,0:T(8,128)S(1)} %cholesky.521), custom_call_target="Cholesky" | custom-call | tf_op jit(solution)/shard_map/jit(cholesky)/cholesky | solution.py:45
  384.3 9.8 %custom-call.60 = f32[1,128,128]{1,2,0:T(8,128)S(1)} custom-call(f32[1,128,128]{2,1,0:T(8,128)S(1)} %get-tuple-element.43), custom_call_target="InvertDiagBlocksLowerTriangular" | custom-call | tf_op jit(solution)/shard_map/jit(cholesky)/cholesky | solution.py:45
  396.0 12.1 %cholesky.469 = f32[128,128]{1,0:T(8,128)S(1)} custom-call(f32[128,128]{1,0:T(8,128)S(1)} %cholesky.526), custom_call_target="Cholesky" | custom-call | tf_op jit(solution)/shard_map/jit(cholesky)/cholesky | solution.py:45
  408.8 9.8 %custom-call.61 = f32[1,128,128]{1,2,0:T(8,128)S(1)} custom-call(f32[1,128,128]{2,1,0:T(8,128)S(1)} %get-tuple-element.40), custom_call_target="InvertDiagBlocksLowerTriangular" | custom-call | tf_op jit(solution)/shard_map/jit(cholesky)/cholesky | solution.py:45
  420.2 11.7 %cholesky.487 = f32[128,128]{1,0:T(8,128)S(1)} custom-call(f32[128,128]{1,0:T(8,128)S(1)} %convolution_subtract_fusion.13), custom_call_target="Cholesky" | custom-call | tf_op jit(solution)/shard_map/jit(cholesky)/cholesky | solution.py:45
  437.1 1.9 select_select_fusion
  439.0 24.8 %while.1 = (s32[]{:T(128)}, f32[896,896]{1,0:T(8,128)}, s32[7,2]{0,1:T(2,128)S(1)}, f32[7,128,128]{2,1,0:T(8,128)}, s32[]{:T(128)}) while((s32[]{:T(128)}, f32[896,896]{1,0:T(8,128)}, s32[7,2]{0,1:T(2,128)S(1)}, f32[7,128,128]{2,1,0:T(8,128)}, s32[]{:T(128)}) %tuple.62), condition=%wide.while_cond, body=%wide.while_body.sunk | while | flops 2 | bytes 132705 | solution.py:11
  439.7 2.9 bitcast_dynamic-update-slice_fusion.2
  443.2 2.9 bitcast_dynamic-update-slice_fusion.2
  446.8 2.9 bitcast_dynamic-update-slice_fusion.2
  450.4 2.9 bitcast_dynamic-update-slice_fusion.2
  453.9 2.9 bitcast_dynamic-update-slice_fusion.2
  457.5 2.9 bitcast_dynamic-update-slice_fusion.2
  461.0 2.8 bitcast_dynamic-update-slice_fusion.2
  463.9 69.7 %custom-call.62 = f32[7,128,128]{1,2,0:T(8,128)S(1)} custom-call(f32[7,128,128]{2,1,0:T(8,128)} %get-tuple-element.9), custom_call_target="InvertDiagBlocksLowerTriangular" | custom-call | tf_op jit(solution)/shard_map/triangular_solve | solution.py:11
  533.6 1.9 constant_dynamic-update-slice_fusion.4
  537.8 1.9 convolution_subtract_fusion.1
  546.5 1.8 convolution_subtract_fusion.3
  558.7 1.9 convolution_subtract_fusion.2
  566.9 18.1 %multiply_convert_fusion = bf16[1024,2048]{1,0:T(8,128)(2,1)} fusion(bf16[1024,2048]{1,0:T(8,128)(2,1)} %param.5, f32[1024]{0:T(1024)S(1)} %convert_subtract_fusion, f32[896,1024]{1,0:T(8,128)} %constant_dynamic-update-slice_fusion.22, bf16[896,2048]{1,0:T(8,128)(2,1)} %all-reduce.9.cloned.1.call-done), kind=kOutput, calls=%fused_computation.4 | convolution fusion | flops 22556966912 | bytes 15732736 | tf_op jit(solution)/shard_map/dot_general | solution.py:47
  585.0 6.5 convolution_bitcast_fusion
  591.6 30.3 %reduce-scatter.3.cloned.1.call-done = f32[128,1024]{0,1:T(8,128)} async-done(((f32[512,1024]{0,1:T(8,128)}), f32[128,1024]{0,1:T(8,128)}) %reduce-scatter.3.cloned.1.call-update) | async-done | bytes 524304 | tf_op jit(solution)/shard_map/reduce_scatter | solution.py:66
  622.0 1.8 multiply_convert_fusion.8
  623.8 49.8 %all-gather.5.cloned.1.call-done = bf16[128,8192]{0,1:T(8,128)(2,1)} async-done(((bf16[128,1024]{0,1:T(8,128)(2,1)}), bf16[128,8192]{0,1:T(8,128)(2,1)}) %all-gather.5.cloned.1.call-update) | async-done | bytes 2097168 | tf_op jit(solution)/shard_map/all_gather | solution.py:70
  673.6 11.9 %convolution_convert_fusion = bf16[1024,8192]{1,0:T(8,128)(2,1)} fusion(bf16[128,1024]{0,1:T(8,128)(2,1)} %multiply_convert_fusion.8, bf16[128,8192]{0,1:T(8,128)(2,1)} %all-gather.5.cloned.1.call-done), kind=kOutput, calls=%fused_computation.2 | convolution fusion | flops 2155872256 | bytes 19136512 | tf_op jit(solution)/shard_map/dot_general | solution.py:68
  685.6 123.6 %reduce-scatter.5.cloned.1.call-done = bf16[1024,2048]{1,0:T(8,128)(2,1)} async-done(((bf16[1024,8192]{1,0:T(8,128)(2,1)}), bf16[1024,2048]{1,0:T(8,128)(2,1)}) %reduce-scatter.5.cloned.1.call-update) | async-done | bytes 4194320 | tf_op jit(solution)/shard_map/reduce_scatter | solution.py:75
  809.2 6.8 convert_multiply_fusion
  (155 shorter events, 80.9 us)
Async XLA Ops:
  7.2 104.3 %all-reduce.5.cloned.1.call-start = ((), (), s32[]{:S(2)}) async-start(), calls=%async_computation.2 | async-start | bytes 7340032 | tf_op jit(solution)/shard_map/psum | solution.py:30
  20.4 5.1 copy-start.5
  21.4 4.9 copy-start.6
  22.5 4.7 copy-start.7
  23.5 4.5 copy-start.8
  24.5 4.4 copy-start.9
  25.5 4.2 copy-start.10
  25.5 5.0 copy-start.11
  31.4 222.4 %all-reduce.7.cloned.1.call-start = ((), (), s32[]{:S(2)}) async-start(), calls=%async_computation.3 | async-start | bytes 6422528 | tf_op jit(solution)/shard_map/psum | solution.py:44
  120.5 1.7 copy-start.4
  122.2 444.7 %all-reduce.9.cloned.1.call-start = ((), (), s32[]{:S(2)}) async-start(), calls=%async_computation.4 | async-start | bytes 7340032 | tf_op jit(solution)/shard_map/psum | solution.py:41
  132.3 4.7 copy-start.13
  136.4 448.6 %all-gather.3.cloned.1.call-start = ((), (), s32[]{:S(2)}) async-start(), calls=%async_computation.5 | async-start | bytes 2359296 | tf_op jit(solution)/shard_map/all_gather | solution.py:59
  137.0 485.0 %reduce-scatter.3.cloned.1.call-start = ((), (), s32[]{:S(2)}) async-start(), calls=%async_computation.6 | async-start | bytes 2621440 | tf_op jit(solution)/shard_map/reduce_scatter | solution.py:66
  253.8 4.7 copy-start
  260.8 1.7 copy-start.3
  287.2 0.7 copy-start.12
  533.6 4.2 copy-start.1
  537.1 3.3 copy-start.2
  591.6 82.1 %all-gather.5.cloned.1.call-start = ((), (), s32[]{:S(2)}) async-start(), calls=%async_computation.7 | async-start | bytes 2359296 | tf_op jit(solution)/shard_map/all_gather | solution.py:70
  623.8 185.4 %reduce-scatter.5.cloned.1.call-start = ((), (), s32[]{:S(2)}) async-start(), calls=%async_computation.8 | async-start | bytes 20971520 | tf_op jit(solution)/shard_map/reduce_scatter | solution.py:75
Sparse Core Ops, SparseCore 0:
  31.5 79.9 all-reduce.4
  122.3 131.4 all-reduce.6
  258.1 141.9 all-reduce.8
  402.1 48.7 all-gather.2
  591.7 30.2 reduce-scatter.2
  624.5 49.0 all-gather.4
  685.7 123.4 reduce-scatter.4
where the time goes:
time: 830 us; the launch traced here: 823 us
  waiting for transfers between devices  397 us (48%)
  other arithmetic  265 us (32%)
  matrix products  79.4 us (10%)
  local copies, waits for them, and re-layouts  53 us (6%)
  between operations  28.5 us (3%)
    another operation x27, other arithmetic, shards(): chol_lower = jnp.linalg.cholesky(inverse_square)  153 us
    reduce_scatter x1, waiting for transfers between devices, shards(): lax.psum_scatter(gram_term.astype(jnp.bfloat16), 'mp', scatter_dimension=...  124 us
    psum x1, waiting for transfers between devices, shards(): inverse_square = lax.psum(jnp.concatenate(inverse_parts, axis=0), 'rows')  117 us
    psum x1, waiting for transfers between devices, shards(): columns = lax.psum(jnp.concatenate(col_pieces, axis=1), 'mp')  75.6 us
    another operation x3, other arithmetic, spd_solve(): lax.linalg.triangular_solve(chol_lower, forward, left_side=True, lower=Tr...  72.3 us
    all_gather x1, waiting for transfers between devices, shards(): lax.all_gather(own_rows, 'rows', axis=1, tiled=True)  49.8 us
    reduce_scatter x1, waiting for transfers between devices, shards(): lax.psum_scatter(partial_value, 'mp', scatter_dimension=0, tiled=True)  30.3 us
    unnamed x19, other arithmetic  24.9 us
  transfers between devices with their start and end apart: 7, of which 5 were waited for; matrix products, arithmetic and copies ran while one was open for 41% of the time, Pallas kernels for 0%

commit v1 on v0

v1 whole, which is shorter than its diff:
```python
import jax
import jax.numpy as jnp
from jax import lax
from jax.experimental import pallas as pl
from jax.experimental.pallas import tpu as pltpu
from jax.sharding import PartitionSpec as P

BLOCK = 128
SUB = 8


def split3(value):
    first = value.astype(jnp.bfloat16)
    rest = value - first.astype(jnp.float32)
    second = rest.astype(jnp.bfloat16)
    third = (rest - second.astype(jnp.float32)).astype(jnp.bfloat16)
    return first, second, third


def sweep_block(tiles):
    lane = lax.broadcasted_iota(jnp.int32, (SUB, BLOCK), 1)
    sublane = lax.broadcasted_iota(jnp.int32, (SUB, BLOCK), 0)
    wide = (SUB, BLOCK)
    for p in range(0, BLOCK, 2):
        q = p + 1
        own, s = p // SUB, p % SUB
        row_p = jnp.broadcast_to(tiles[own][s : s + 1, :], wide)
        row_q = jnp.broadcast_to(tiles[own][s + 1 : s + 2, :], wide)
        d_p = jnp.broadcast_to(row_p[:, p : p + 1], wide)
        off = jnp.broadcast_to(row_p[:, q : q + 1], wide)
        d_q = jnp.broadcast_to(row_q[:, q : q + 1], wide)
        inv_p = 1.0 / d_p
        ratio = off * inv_p
        m_qq = 1.0 / (d_q - off * ratio)
        m_pq = -ratio * m_qq
        m_pp = inv_p - ratio * m_pq
        is_p, is_q = lane == p, lane == q
        u_p = m_pp * row_p + m_pq * row_q
        u_q = m_pq * row_p + m_qq * row_q
        u_p = jnp.where(is_p, -m_pp, jnp.where(is_q, -m_pq, u_p))
        u_q = jnp.where(is_p, -m_pq, jnp.where(is_q, -m_qq, u_q))
        pivot = is_p | is_q
        new = []
        for t in range(len(tiles)):
            col_p = jnp.broadcast_to(tiles[t][:, p : p + 1], wide)
            col_q = jnp.broadcast_to(tiles[t][:, q : q + 1], wide)
            value = jnp.where(pivot, 0.0, tiles[t]) - col_p * u_p - col_q * u_q
            if t == own:
                value = jnp.where(sublane == s, u_p, jnp.where(sublane == s + 1, u_q, value))
            new.append(value)
        tiles = new
    return tiles


def invert_kernel(low_ref, out_ref, neg_ref, rhs_ref, pivot_ref):
    count = out_ref.shape[0] // BLOCK
    at = 0
    for i in range(count):
        for j in range(i + 1):
            block = low_ref[:, at : at + BLOCK]
            at += BLOCK
            out_ref[i * BLOCK : (i + 1) * BLOCK, j * BLOCK : (j + 1) * BLOCK] = block
            if j < i:
                out_ref[j * BLOCK : (j + 1) * BLOCK, i * BLOCK : (i + 1) * BLOCK] = block.T

    def stage(k, carry):
        here = pl.ds(pl.multiple_of(k * BLOCK, BLOCK), BLOCK)
        diag = out_ref[here, here]
        tiles = [diag[t * SUB : (t + 1) * SUB, :] for t in range(BLOCK // SUB)]
        tiles = sweep_block(tiles)
        for t in range(BLOCK // SUB):
            neg_ref[t * SUB : (t + 1) * SUB, :] = tiles[t]
        neg = neg_ref[...]
        r1, r2, r3 = split3(out_ref[here, :])
        a1, a2, a3 = split3(-neg)
        pivot_ref[...] = jnp.dot(
            jnp.concatenate([a1, a1, a2, a2, a1, a3], axis=1),
            jnp.concatenate([r1, r2, r1, r2, r3, r1], axis=0),
            preferred_element_type=jnp.float32,
        )
        pivot_ref[:, here] = neg
        b1, b2, b3 = split3(pivot_ref[...])
        for slot, part in enumerate((b1, b2, b1, b2, b3, b1)):
            rhs_ref[slot * BLOCK : (slot + 1) * BLOCK, :] = part

        def update(i, inner):
            rows = pl.ds(pl.multiple_of(i * BLOCK, BLOCK), BLOCK)
            c1, c2, c3 = split3(out_ref[rows, here])
            out_ref[rows, here] = jnp.zeros((BLOCK, BLOCK), jnp.float32)
            out_ref[rows, :] -= jnp.dot(
                jnp.concatenate([c1, c1, c2, c2, c1, c3], axis=1),
                rhs_ref[...],
                preferred_element_type=jnp.float32,
            )
            return inner

        lax.fori_loop(0, count, update, 0)
        out_ref[here, :] = pivot_ref[...]
        return carry

    lax.fori_loop(0, count, stage, 0)


def minus_inverse(low, order):
    vmem = pl.BlockSpec(memory_space=pltpu.VMEM)
    return pl.pallas_call(
        invert_kernel,
        out_shape=jax.ShapeDtypeStruct((order, order), jnp.float32),
        in_specs=[vmem],
        out_specs=vmem,
        scratch_shapes=[
            pltpu.VMEM((BLOCK, BLOCK), jnp.float32),
            pltpu.VMEM((6 * BLOCK, order), jnp.bfloat16),
            pltpu.VMEM((BLOCK, order), jnp.float32),
        ],
        compiler_params=pltpu.CompilerParams(vmem_limit_bytes=32 * 1024 * 1024),
        cost_estimate=pl.CostEstimate(
            flops=60_000_000_000, bytes_accessed=2 * order * order * 4, transcendentals=0
        ),
    )(low)


def shards(calib, weight, inverse_factor, pruned_blocks):
    rows_dev = weight.shape[0]
    width_dev = weight.shape[1]
    row_parts = lax.axis_size("rows")
    mp_parts = lax.axis_size("mp")
    full_width = width_dev * mp_parts
    row_start = lax.axis_index("rows") * rows_dev
    col_start = lax.axis_index("mp") * width_dev
    starts = pruned_blocks * BLOCK
    block_count = pruned_blocks.shape[0]
    col_pieces = []
    for slot_index in range(block_count):
        offset = starts[slot_index] - col_start
        inside = (offset >= 0) & (offset < width_dev)
        clamped = jnp.clip(offset, 0, width_dev - BLOCK)
        piece = lax.dynamic_slice_in_dim(inverse_factor, clamped, BLOCK, 1)
        col_pieces.append(jnp.where(inside, piece, 0.0))
    columns = jnp.concatenate(col_pieces, axis=1)
    weight_parts = []
    low_parts = []
    for slot_index in range(block_count):
        offset = starts[slot_index] - row_start
        inside = (offset >= 0) & (offset < rows_dev)
        clamped = jnp.clip(offset, 0, rows_dev - BLOCK)
        piece = lax.dynamic_slice_in_dim(weight, clamped, BLOCK, 0)
        weight_parts.append(jnp.where(inside, piece, jnp.zeros_like(piece)))
        piece = lax.dynamic_slice(columns, (clamped, 0), (BLOCK, (slot_index + 1) * BLOCK))
        low_parts.append(jnp.where(inside, piece, 0.0))
    low = lax.psum(jnp.concatenate(low_parts, axis=1), ("rows", "mp"))
    own_columns = lax.psum_scatter(columns, "mp", scatter_dimension=0, tiled=True)
    kept_rows = lax.psum(jnp.concatenate(weight_parts, axis=0), "rows")
    all_calib = lax.all_gather(calib, "rows", axis=0, tiled=True)

    negative = minus_inverse(low, block_count * BLOCK)
    own_factors = -lax.dot_general(
        own_columns,
        negative,
        (((1,), (0,)), ((), ())),
        precision=lax.Precision.HIGHEST,
        preferred_element_type=jnp.float32,
    )
    factors = lax.all_gather(own_factors.astype(jnp.bfloat16), "mp", axis=0, tiled=True)
    update = lax.dot_general(
        factors, kept_rows, (((1,), (0,)), ((), ())), preferred_element_type=jnp.float32
    )
    block_ids = (row_start + jnp.arange(rows_dev, dtype=jnp.int32)) // BLOCK
    pruned = jnp.any(block_ids[:, None] == pruned_blocks[None, :], axis=1)
    pruned_weight = jnp.where(
        pruned[:, None], 0.0, weight.astype(jnp.float32) - update
    ).astype(jnp.bfloat16)
    out_scale = float(full_width) ** (-0.5)
    partial_value = lax.dot_general(
        all_calib, pruned_weight, (((1,), (1,)), ((), ())), preferred_element_type=jnp.float32
    )
    token_count = partial_value.shape[0]
    own_rows = lax.psum_scatter(
        (partial_value * out_scale).astype(jnp.bfloat16), "mp", scatter_dimension=0, tiled=True
    )
    per_col = row_parts // mp_parts
    pairs = []
    for r in range(row_parts):
        for m in range(mp_parts):
            target = ((r % per_col) * mp_parts + m) * mp_parts + r // per_col
            pairs.append((r * mp_parts + m, target))
    moved = lax.ppermute(own_rows, ("rows", "mp"), pairs)
    left = lax.all_gather(own_rows, "mp", axis=0, tiled=True)
    right = lax.all_gather(moved, "rows", axis=0, tiled=False)
    right = right.reshape(per_col, token_count, rows_dev)
    gram_pieces = [
        lax.dot_general(
            left, right[c], (((0,), (0,)), ((), ())), preferred_element_type=jnp.float32
        )
        for c in range(per_col)
    ]
    gram_block = jnp.concatenate(gram_pieces, axis=1) / token_count
    return (pruned_weight, gram_block)


def solution(mesh):
    return jax.shard_map(
        shards,
        mesh=mesh,
        in_specs=(P("rows", "mp"), P("rows", "mp"), P("rows", "mp"), P()),
        out_specs=(P("rows", "mp"), P("rows", "mp")),
        check_vma=False,
    )
```

time: 830 us -> 502 us (0.60)
  other arithmetic: 265 us -> 40.7 us
  waiting for transfers between devices: 397 us -> 291 us
  Pallas kernels: 0 us -> 100 us
  matrix products: 79.4 us -> 25.4 us
  local copies, waits for them, and re-layouts: 53 us -> 16.4 us
    another operation x30 -> x0, other arithmetic: 226 us -> none  [the longest x27 153 us: shards(): chol_lower = jnp.linalg.cholesky(inverse_square)]
    reduce_scatter x2 -> x1, waiting for transfers between devices: 154 us -> 0.03 us  [shards(): lax.psum_scatter(columns, 'mp', scatter_dimension=0, tiled=True)]
    pallas_call x0 -> x1, Pallas kernels: none -> 100 us  [minus_inverse(): pl.pallas_call(invert_kernel, out_shape=jax.ShapeDtypeStruct((order, orde...]
    all_gather x2 -> x4, waiting for transfers between devices: 49.8 us -> 100 us  [the longest x1 54.8 us: shards(): right = lax.all_gather(moved, 'rows', axis=0, tiled=False)]
    another operation x38 -> x0, matrix products: 42.8 us -> none  [the longest x13 15.2 us: spd_solve(): lax.linalg.triangular_solve(chol_lower, right_side, left_side=True, lower...]
    another operation x32 -> x0, local copies, waits for them, and re-layouts: 26.6 us -> none
    psum x3 -> x2, waiting for transfers between devices: 192 us -> 166 us  [the longest x1 128 us: shards(): low = lax.psum(jnp.concatenate(low_parts, axis=1), ('rows', 'mp'))]
    unnamed x7 -> x9, waiting for transfers between devices: 0.62 us -> 24.5 us
  transfers between devices with their start and end apart: 7 -> 9, of which waited for: 5 -> 6; matrix products, arithmetic and copies ran while one was open for 41% -> 6% of each run, Pallas kernels for 0% -> 20%
where the time goes in v1:
time: 502 us; the launch traced here: 501 us
  waiting for transfers between devices  291 us (58%)
  Pallas kernels  100 us (20%)
  other arithmetic  40.7 us (8%)
  matrix products  25.4 us (5%)
  between operations  24.7 us (5%)
  local copies, waits for them, and re-layouts  16.4 us (3%)
    psum x1, waiting for transfers between devices, shards(): low = lax.psum(jnp.concatenate(low_parts, axis=1), ('rows', 'mp'))  128 us
    pallas_call x1, Pallas kernels, minus_inverse(): pl.pallas_call(invert_kernel, out_shape=jax.ShapeDtypeStruct((order, orde...  100 us
    all_gather x1, waiting for transfers between devices, shards(): right = lax.all_gather(moved, 'rows', axis=0, tiled=False)  54.8 us
    psum x1, waiting for transfers between devices, shards(): kept_rows = lax.psum(jnp.concatenate(weight_parts, axis=0), 'rows')  38.3 us
    unnamed x18, other arithmetic  30.6 us
    all_gather x1, waiting for transfers between devices, shards(): all_calib = lax.all_gather(calib, 'rows', axis=0, tiled=True)  25.6 us
    unnamed x9, waiting for transfers between devices  24.5 us
    all_gather x1, waiting for transfers between devices, shards(): left = lax.all_gather(own_rows, 'mp', axis=0, tiled=True)  20.1 us
  transfers between devices with their start and end apart: 9, of which 6 were waited for; matrix products, arithmetic and copies ran while one was open for 6% of the time, Pallas kernels for 20%

profile of v1, /device:TPU:0, one launch (start us, length us, event | category | flops | bytes accessed | tf_op | source)
XLA Modules:
  0.0 500.9 jit_solution(5189823947785905863)
XLA Ops:
  8.0 0.7 broadcast_multiply_fusion
  8.7 0.7 fusion.9
  18.4 2.0 select_dynamic-update-slice_fusion.13
  20.4 2.0 select_dynamic-update-slice_fusion.12
  22.5 2.0 select_dynamic-update-slice_fusion.11
  24.5 2.2 select_dynamic-update-slice_fusion.10
  26.7 2.2 select_dynamic-update-slice_fusion.9
  28.9 2.2 select_dynamic-update-slice_fusion.8
  31.2 2.0 select_dynamic-update-slice_fusion.7
  33.2 0.9 select_dynamic-update-slice_fusion.20
  34.1 0.9 select_dynamic-update-slice_fusion.19
  35.0 1.0 select_dynamic-update-slice_fusion.18
  36.0 1.0 select_dynamic-update-slice_fusion.17
  37.0 1.0 select_dynamic-update-slice_fusion.16
  38.0 1.1 select_dynamic-update-slice_fusion.15
  39.1 1.1 select_dynamic-update-slice_fusion.14
  40.2 1.2 copy-done.3
  41.5 0.5 reduce-scatter.5.cloned.1.call-update
  42.1 2.0 select_dynamic-update-slice_fusion.6
  44.1 2.0 select_dynamic-update-slice_fusion.5
  46.1 2.0 select_dynamic-update-slice_fusion.4
  48.1 2.0 select_dynamic-update-slice_fusion.3
  50.1 2.0 select_dynamic-update-slice_fusion.2
  52.1 2.0 select_dynamic-update-slice_fusion.1
  54.1 2.0 select_dynamic-update-slice_fusion
  56.1 0.2 all-gather.6.cloned.1.call-start
  56.3 127.9 %all-reduce.3.cloned.1.call-done.low_ref = f32[128,3584]{1,0:T(8,128)} async-done(((f32[128,3584]{1,0:T(8,128)}), f32[128,3584]{1,0:T(8,128)}) %all-reduce.3.cloned.1.call-update) | async-done | bytes 1835024 | tf_op jit(solution)/shard_map/psum | solution.py:151
  184.3 1.5 copy-done
  185.8 100.1 %shard_map.59 = f32[896,896]{1,0:T(8,128)S(1)} custom-call(f32[128,3584]{1,0:T(8,128)S(1)} %copy-done), custom_call_target="tpu_custom_call" | custom-call | flops 60000002048 | bytes 6422528 | tf_op jit(solution)/shard_map/pallas_call | solution.py:106
  285.9 5.5 %fusion.1 = bf16[256,896]{1,0:T(8,128)(2,1)} fusion(f32[256,896]{1,0:T(8,128)} %reduce-scatter.5.cloned.1.call-done, f32[896,896]{1,0:T(8,128)S(1)} %shard_map.59), kind=kOutput, calls=%fused_computation.5 | convolution fusion | flops 2466709504 | bytes 4587520 | tf_op jit(solution)/shard_map/dot_general | solution.py:157
  291.6 0.5 all-gather.8.cloned.1.call-update
  292.1 0.3 reduce-scatter.7.cloned.1.call-start
  292.4 0.1 compare_reduce_fusion
  292.5 38.3 %all-reduce.5.cloned.1.call-done = bf16[896,2048]{1,0:T(8,128)(2,1)} async-done(((bf16[896,2048]{1,0:T(8,128)(2,1)}), bf16[896,2048]{1,0:T(8,128)(2,1)}) %all-reduce.5.cloned.1.call-update) | async-done | bytes 3670032 | tf_op jit(solution)/shard_map/psum | solution.py:153
  330.8 10.4 %select_convert_fusion = bf16[1024,2048]{1,0:T(8,128)(2,1)} fusion(bf16[1024,2048]{1,0:T(8,128)(2,1)} %param.5, pred[1024]{0:T(1024)(128)(4,1)S(1)} %compare_reduce_fusion, bf16[1024,896]{1,0:T(8,128)(2,1)} %all-gather.6.cloned.1.call-done, bf16[896,2048]{1,0:T(8,128)(2,1)} %all-reduce.5.cloned.1.call-done), kind=kOutput, calls=%fused_computation.1 | convolution fusion | flops 3766484992 | bytes 13894656 | tf_op jit(solution)/shard_map/dot_general | solution.py:165
  341.2 25.6 %all-gather.8.cloned.1.call-done = bf16[512,2048]{1,0:T(8,128)(2,1)} async-done(((bf16[64,2048]{1,0:T(8,128)(2,1)}), bf16[512,2048]{1,0:T(8,128)(2,1)}) %all-gather.8.cloned.1.call-update) | async-done | bytes 2097168 | tf_op jit(solution)/shard_map/all_gather | solution.py:154
  366.8 5.2 %fusion = bf16[512,1024]{0,1:T(8,128)(2,1)S(1)} fusion(bf16[1024,2048]{1,0:T(8,128)(2,1)} %select_convert_fusion, bf16[512,2048]{1,0:T(8,128)(2,1)} %all-gather.8.cloned.1.call-done), kind=kOutput, calls=%fused_computation.3 | convolution fusion | flops 2148532224 | bytes 7340032 | tf_op jit(solution)/shard_map/dot_general | solution.py:174
  372.0 1.3 copy.9
  373.4 23.4 %reduce-scatter.7.cloned.1.call-done = bf16[128,1024]{1,0:T(8,128)(2,1)} async-done(((bf16[512,1024]{1,0:T(8,128)(2,1)}), bf16[128,1024]{1,0:T(8,128)(2,1)}) %reduce-scatter.7.cloned.1.call-update) | async-done | bytes 262160
  396.8 1.8 copy.10
  398.7 1.6 collective-permute-start
  400.3 0.7 copy-done.4
  401.0 20.1 %all-gather.10.cloned.1.call-done = bf16[512,1024]{0,1:T(8,128)(2,1)} async-done(((bf16[128,1024]{0,1:T(8,128)(2,1)}), bf16[512,1024]{0,1:T(8,128)(2,1)}) %all-gather.10.cloned.1.call-update) | async-done | bytes 1048592 | tf_op jit(solution)/shard_map/all_gather | solution.py:188
  421.1 54.8 %all-gather.12.cloned.1.call-done = bf16[1024,1024]{0,1:T(8,128)(2,1)} async-done(((bf16[128,1024]{0,1:T(8,128)(2,1)}), bf16[1024,1024]{0,1:T(8,128)(2,1)}) %all-gather.12.cloned.1.call-update) | async-done | bytes 2097168 | tf_op jit(solution)/shard_map/all_gather | solution.py:189
  475.8 3.0 fusion.4
  478.8 1.3 fusion.2
  480.1 4.2 maximum_multiply_fusion
  484.3 9.1 %copy.8 = f32[1024,2048]{1,0:T(8,128)} copy(f32[1024,2048]{0,1:T(8,128)} %maximum_multiply_fusion) | data formatting | bytes 16777216
  (25 shorter events, 0.4 us)
Async XLA Ops:
  8.0 176.3 %all-reduce.3.cloned.1.call-start = ((), (), s32[]{:S(2)}) async-start(), calls=%async_computation.3 | async-start | bytes 3670016 | tf_op jit(solution)/shard_map/psum | solution.py:151
  40.2 1.3 copy-start.3
  41.4 244.5 %reduce-scatter.5.cloned.1.call-start = ((), (), s32[]{:S(2)}) async-start(), calls=%async_computation.2 | async-start | bytes 4587520 | tf_op jit(solution)/shard_map/reduce_scatter | solution.py:152
  42.0 288.8 %all-reduce.5.cloned.1.call-start = ((), (), s32[]{:S(2)}) async-start(), calls=%async_computation.5 | async-start | bytes 7340032 | tf_op jit(solution)/shard_map/psum | solution.py:153
  56.1 274.6 %all-gather.6.cloned.1.call-start = ((), (), s32[]{:S(2)}) async-start(), calls=%async_computation.4 | async-start | bytes 2293760 | tf_op jit(solution)/shard_map/all_gather | solution.py:164
  184.3 1.5 copy-start
  285.9 6.5 %copy-start.5 = (s32[7]{0:T(128)S(1)}, s32[7]{0:T(128)}, u32[]{:S(2)}) copy-start(s32[7]{0:T(128)} %param.7) | copy-start | bytes 88
  291.5 75.3 %all-gather.8.cloned.1.call-start = ((), (), s32[]{:S(2)}) async-start(), calls=%async_computation.6 | async-start | bytes 2359296 | tf_op jit(solution)/shard_map/all_gather | solution.py:154
  292.1 104.7 %reduce-scatter.7.cloned.1.call-start = ((), (), s32[]{:S(2)}) async-start(), calls=%async_computation.9 | async-start | bytes 1310720
  373.4 47.7 %all-gather.10.cloned.1.call-start = ((), (), s32[]{:S(2)}) async-start(), calls=%async_computation.7 | async-start | bytes 1310720 | tf_op jit(solution)/shard_map/all_gather | solution.py:188
  398.6 77.2 %all-gather.12.cloned.1.call-start = ((), (), s32[]{:S(2)}) async-start(), calls=%async_computation.8 | async-start | bytes 2359296 | tf_op jit(solution)/shard_map/all_gather | solution.py:189
  398.7 1.6 collective-permute-start
  400.3 0.7 copy-start.4
  421.1 57.7 %copy-start.1 = (bf16[512,1024]{0,1:T(8,128)(2,1)S(1)}, bf16[512,1024]{0,1:T(8,128)(2,1)}, u32[]{:S(2)}) copy-start(bf16[512,1024]{0,1:T(8,128)(2,1)} %all-gather.10.cloned.1.call-done) | copy-start | bytes 3145732
  475.8 3.0 copy-start.2
Sparse Core Ops, SparseCore 0:
  41.6 142.6 all-reduce.2
  188.5 142.1 all-reduce.4
Sparse Core Ops, SparseCore 1:
  45.0 44.8 reduce-scatter.4
  291.6 19.8 all-gather.5
  313.5 53.2 all-gather.7
  373.4 23.3 reduce-scatter.6
  398.9 22.1 all-gather.9
  423.1 52.6 all-gather.11

commit v2 on v1

--- a/solution.py
+++ b/solution.py
@@ -1,3 +1,5 @@
+import functools
+
 import jax
 import jax.numpy as jnp
 from jax import lax
@@ -120,6 +122,86 @@
     )(low)
 
 
+def pick_columns_kernel(places_ref, factor_ref, columns_ref, low_ref):
+    j = pl.program_id(0)
+    columns_ref[...] = jnp.where(places_ref[1, j] != 0, factor_ref[...], 0.0)
+    for i in range(places_ref.shape[1]):
+
+        @pl.when(i >= j)
+        def _():
+            rows = pl.ds(pl.multiple_of(places_ref[2, i] * BLOCK, BLOCK), BLOCK)
+            lanes = pl.ds(pl.multiple_of((i * (i + 1) // 2 + j) * BLOCK, BLOCK), BLOCK)
+            low_ref[:, lanes] = jnp.where(places_ref[3, i] != 0, columns_ref[rows, :], 0.0)
+
+
+def pick_columns(places, factor):
+    count = places.shape[1]
+    rows = factor.shape[0]
+    lanes = count * (count + 1) // 2 * BLOCK
+    return pl.pallas_call(
+        pick_columns_kernel,
+        out_shape=(
+            jax.ShapeDtypeStruct((rows, count * BLOCK), jnp.float32),
+            jax.ShapeDtypeStruct((BLOCK, lanes), jnp.float32),
+        ),
+        grid_spec=pltpu.PrefetchScalarGridSpec(
+            num_scalar_prefetch=1,
+            grid=(count,),
+            in_specs=[pl.BlockSpec((rows, BLOCK), lambda j, places: (0, places[0, j]))],
+            out_specs=(
+                pl.BlockSpec((rows, BLOCK), lambda j, places: (0, j)),
+                pl.BlockSpec((BLOCK, lanes), lambda j, places: (0, 0)),
+            ),
+        ),
+    )(places, factor)
+
+
+def pick_rows_kernel(places_ref, weight_ref, out_ref):
+    inside = places_ref[3, pl.program_id(0)] != 0
+    value = weight_ref[...].astype(jnp.float32)
+    out_ref[...] = jnp.where(inside, value, 0.0).astype(jnp.bfloat16)
+
+
+def pick_rows(places, weight):
+    count = places.shape[1]
+    width = weight.shape[1]
+    return pl.pallas_call(
+        pick_rows_kernel,
+        out_shape=jax.ShapeDtypeStruct((count * BLOCK, width), jnp.bfloat16),
+        grid_spec=pltpu.PrefetchScalarGridSpec(
+            num_scalar_prefetch=1,
+            grid=(count,),
+            in_specs=[pl.BlockSpec((BLOCK, width), lambda i, places: (places[2, i], 0))],
+            out_specs=pl.BlockSpec((BLOCK, width), lambda i, places: (i, 0)),
+        ),
+    )(places, weight)
+
+
+def gram_kernel(token_count, left_ref, right_ref, out_ref):
+    out_ref[...] = lax.dot_general(
+        left_ref[...],
+        right_ref[0],
+        (((0,), (0,)), ((), ())),
+        preferred_element_type=jnp.float32,
+    ) / token_count
+
+
+def gram_of(left, right, token_count):
+    tokens, rows = left.shape
+    parts, _, width = right.shape
+    tile = min(rows, 256)
+    return pl.pallas_call(
+        functools.partial(gram_kernel, token_count),
+        grid=(parts, rows // tile),
+        in_specs=[
+            pl.BlockSpec((tokens, tile), lambda c, i: (0, i)),
+            pl.BlockSpec((1, tokens, width), lambda c, i: (c, 0, 0)),
+        ],
+        out_specs=pl.BlockSpec((tile, width), lambda c, i: (i, c)),
+        out_shape=jax.ShapeDtypeStruct((rows, parts * width), jnp.float32),
+    )(left, right)
+
+
 def shards(calib, weight, inverse_factor, pruned_blocks):
     rows_dev = weight.shape[0]
     width_dev = weight.shape[1]
@@ -130,30 +212,26 @@
     col_start = lax.axis_index("mp") * width_dev
     starts = pruned_blocks * BLOCK
     block_count = pruned_blocks.shape[0]
-    col_pieces = []
-    for slot_index in range(block_count):
-        offset = starts[slot_index] - col_start
-        inside = (offset >= 0) & (offset < width_dev)
-        clamped = jnp.clip(offset, 0, width_dev - BLOCK)
-        piece = lax.dynamic_slice_in_dim(inverse_factor, clamped, BLOCK, 1)
-        col_pieces.append(jnp.where(inside, piece, 0.0))
-    columns = jnp.concatenate(col_pieces, axis=1)
-    weight_parts = []
-    low_parts = []
-    for slot_index in range(block_count):
-        offset = starts[slot_index] - row_start
-        inside = (offset >= 0) & (offset < rows_dev)
-        clamped = jnp.clip(offset, 0, rows_dev - BLOCK)
-        piece = lax.dynamic_slice_in_dim(weight, clamped, BLOCK, 0)
-        weight_parts.append(jnp.where(inside, piece, jnp.zeros_like(piece)))
-        piece = lax.dynamic_slice(columns, (clamped, 0), (BLOCK, (slot_index + 1) * BLOCK))
-        low_parts.append(jnp.where(inside, piece, 0.0))
-    low = lax.psum(jnp.concatenate(low_parts, axis=1), ("rows", "mp"))
+    col_offsets = starts - col_start
+    row_offsets = starts - row_start
+    places = jnp.stack(
+        [
+            jnp.clip(col_offsets, 0, width_dev - BLOCK) // BLOCK,
+            ((col_offsets >= 0) & (col_offsets < width_dev)).astype(jnp.int32),
+            jnp.clip(row_offsets, 0, rows_dev - BLOCK) // BLOCK,
+            ((row_offsets >= 0) & (row_offsets < rows_dev)).astype(jnp.int32),
+        ]
+    ).astype(jnp.int32)
+    columns, own_low = pick_columns(places, inverse_factor)
+    low = lax.psum(own_low, ("rows", "mp"))
     own_columns = lax.psum_scatter(columns, "mp", scatter_dimension=0, tiled=True)
-    kept_rows = lax.psum(jnp.concatenate(weight_parts, axis=0), "rows")
+    own_kept = pick_rows(places, weight)
+    low, own_kept, calib = lax.optimization_barrier((low, own_kept, calib))
+    kept_rows = lax.psum(own_kept, "rows")
     all_calib = lax.all_gather(calib, "rows", axis=0, tiled=True)
 
     negative = minus_inverse(low, block_count * BLOCK)
+    negative, all_calib, own_columns = lax.optimization_barrier((negative, all_calib, own_columns))
     own_factors = -lax.dot_general(
         own_columns,
         negative,
@@ -188,13 +266,7 @@
     left = lax.all_gather(own_rows, "mp", axis=0, tiled=True)
     right = lax.all_gather(moved, "rows", axis=0, tiled=False)
     right = right.reshape(per_col, token_count, rows_dev)
-    gram_pieces = [
-        lax.dot_general(
-            left, right[c], (((0,), (0,)), ((), ())), preferred_element_type=jnp.float32
-        )
-        for c in range(per_col)
-    ]
-    gram_block = jnp.concatenate(gram_pieces, axis=1) / token_count
+    gram_block = gram_of(left, right, token_count)
     return (pruned_weight, gram_block)
 
 

time: 502 us -> 481 us (0.958)
  other arithmetic: 40.7 us -> 2.03 us
  waiting for transfers between devices: 291 us -> 317 us
  Pallas kernels: 100 us -> 122 us
  local copies, waits for them, and re-layouts: 16.4 us -> 4.21 us
  between operations: 24.7 us -> 15.6 us
  matrix products: 25.4 us -> 17.2 us
    psum x2, waiting for transfers between devices: 166 us -> 218 us  [the longest x1 131 us: shards(): low = lax.psum(own_low, ('rows', 'mp'))]
    unnamed x18 -> x0, other arithmetic: 30.6 us -> none
    all_gather x1, waiting for transfers between devices: 25.6 us -> 0.02 us  [shards(): all_calib = lax.all_gather(calib, 'rows', axis=0, tiled=True)]
    reduce_scatter x0 -> x1, waiting for transfers between devices: none -> 23.6 us  [shards(): lax.psum_scatter((partial_value * out_scale).astype(jnp.bfloat16), 'mp',...]
    unnamed x9 -> x8, waiting for transfers between devices: 24.5 us -> 1.3 us
    pallas_call x0 -> x3, Pallas kernels: none -> 21.6 us  [the longest x1 8.94 us: gram_of(): pl.pallas_call(functools.partial(gram_kernel, token_count), grid=(parts,...]
    unnamed x15 -> x10, local copies, waits for them, and re-layouts: 15.7 us -> 4.21 us
    concatenate x3 -> x0, other arithmetic: 5.13 us -> none  [the longest x1 2.04 us: shards(): columns = jnp.concatenate(col_pieces, axis=1)]
  transfers between devices with their start and end apart: 9 -> 9, of which waited for: 6 -> 5; matrix products, arithmetic and copies ran while one was open for 6% -> 1% of each run, Pallas kernels for 20% -> 22%
where the time goes in v2:
time: 481 us; the launch traced here: 480 us
  waiting for transfers between devices  317 us (66%)
  Pallas kernels  122 us (25%)
  matrix products  17.2 us (4%)
  between operations  15.6 us (3%)
    psum x1, waiting for transfers between devices, shards(): low = lax.psum(own_low, ('rows', 'mp'))  131 us
    pallas_call x1, Pallas kernels, minus_inverse(): pl.pallas_call(invert_kernel, out_shape=jax.ShapeDtypeStruct((order, orde...  100 us
    psum x1, waiting for transfers between devices, shards(): kept_rows = lax.psum(own_kept, 'rows')  87.1 us
    all_gather x1, waiting for transfers between devices, shards(): right = lax.all_gather(moved, 'rows', axis=0, tiled=False)  53.8 us
    reduce_scatter x1, waiting for transfers between devices, shards(): lax.psum_scatter((partial_value * out_scale).astype(jnp.bfloat16), 'mp',...  23.6 us
    all_gather x1, waiting for transfers between devices, shards(): left = lax.all_gather(own_rows, 'mp', axis=0, tiled=True)  20.1 us
  transfers between devices with their start and end apart: 9, of which 5 were waited for; matrix products, arithmetic and copies ran while one was open for 1% of the time, Pallas kernels for 22%

profile of v2, /device:TPU:0, one launch (start us, length us, event | category | flops | bytes accessed | tf_op | source)
XLA Modules:
  0.0 480.0 jit_solution(4642458449996068674)
XLA Ops:
  8.0 0.0 all-reduce.3.cloned.1.call-start
  8.0 0.7 fusion.4
  8.7 0.7 fusion.7
  9.4 0.6 pad_add_fusion.places_ref
  10.0 6.7 %shard_map.59 = (f32[1024,896]{1,0:T(8,128)}, f32[128,3584]{1,0:T(8,128)}) custom-call(s32[4,7]{1,0:T(4,128)} %pad_add_fusion.places_ref, f32[1024,2048]{1,0:T(8,128)} %factor_ref.1), custom_call_target="tpu_custom_call" | custom-call | tf_op jit(solution)/shard_map/pallas_call | solution.py:141
  16.7 0.0 all-reduce.3.cloned.1.call-update
  16.8 0.0 all-gather.6.cloned.1.call-start
  16.8 5.9 %shard_map.60 = bf16[896,2048]{1,0:T(8,128)(2,1)} custom-call(s32[4,7]{1,0:T(4,128)} %pad_add_fusion.places_ref, bf16[1024,2048]{1,0:T(8,128)(2,1)} %weight_ref.1), custom_call_target="tpu_custom_call" | custom-call | tf_op jit(solution)/shard_map/pallas_call | solution.py:168
  22.7 131.1 %all-reduce.3.cloned.1.call-done.low_ref = f32[128,3584]{1,0:T(8,128)} async-done(((f32[128,3584]{1,0:T(8,128)}), f32[128,3584]{1,0:T(8,128)}) %all-reduce.3.cloned.1.call-update) | async-done | bytes 1835024 | tf_op jit(solution)/shard_map/psum | solution.py:226
  153.8 0.0 all-gather.6.cloned.1.call-update
  153.9 0.0 reduce-scatter.3.cloned.1.call-start
  153.9 0.5 reduce-scatter.3.cloned.1.call-update
  154.4 0.0 all-reduce.5.cloned.1.call-start
  154.5 0.7 all-reduce.5.cloned.1.call-update
  155.2 0.0 all-gather.8.cloned.1.call-start
  155.2 0.0 copy-start
  155.2 1.5 copy-done
  156.7 100.2 %shard_map.61 = f32[896,896]{1,0:T(8,128)S(1)} custom-call(f32[128,3584]{1,0:T(8,128)S(1)} %copy-done), custom_call_target="tpu_custom_call" | custom-call | flops 60000002048 | bytes 6422528 | tf_op jit(solution)/shard_map/pallas_call | solution.py:108
  256.9 0.0 copy-start.2
  256.9 0.0 all-gather.6.cloned.1.call-done
  256.9 0.0 reduce-scatter.3.cloned.1.call-done
  257.0 5.5 %fusion = bf16[256,896]{1,0:T(8,128)(2,1)} fusion(f32[256,896]{1,0:T(8,128)} %reduce-scatter.3.cloned.1.call-done, f32[896,896]{1,0:T(8,128)S(1)} %shard_map.61), kind=kOutput, calls=%fused_computation.3 | convolution fusion | flops 2466709504 | bytes 4587520 | tf_op jit(solution)/shard_map/dot_general | solution.py:235
  262.5 0.0 all-gather.8.cloned.1.call-update
  262.5 0.2 reduce-scatter.5.cloned.1.call-start
  262.8 0.0 copy-done.2
  262.8 0.1 compare_reduce_fusion
  262.9 0.0 copy-start.3
  262.9 87.1 %all-reduce.5.cloned.1.call-done = bf16[896,2048]{1,0:T(8,128)(2,1)} async-done(((bf16[896,2048]{1,0:T(8,128)(2,1)}), bf16[896,2048]{1,0:T(8,128)(2,1)}) %all-reduce.5.cloned.1.call-update) | async-done | bytes 3670032 | tf_op jit(solution)/shard_map/psum | solution.py:230
  350.0 0.0 all-gather.8.cloned.1.call-done
  350.0 8.4 %select_convert_fusion = bf16[1024,2048]{1,0:T(8,128)(2,1)S(1)} fusion(bf16[1024,2048]{1,0:T(8,128)(2,1)} %weight_ref.1, pred[1024]{0:T(1024)(128)(4,1)S(1)} %compare_reduce_fusion, bf16[1024,896]{1,0:T(8,128)(2,1)} %all-gather.8.cloned.1.call-done, bf16[896,2048]{1,0:T(8,128)(2,1)} %all-reduce.5.cloned.1.call-done), kind=kOutput, calls=%fused_computation | convolution fusion | flops 3766484992 | bytes 13894656 | tf_op jit(solution)/shard_map/dot_general | solution.py:243
  358.3 0.0 copy-start.4
  358.4 2.0 copy-done.4
  360.4 0.0 copy-done.3
  360.4 3.4 multiply_convert_fusion
  363.7 0.0 reduce-scatter.5.cloned.1.call-update
  363.8 0.0 all-gather.10.cloned.1.call-start
  363.8 23.6 %reduce-scatter.5.cloned.1.call-done = bf16[128,1024]{1,0:T(8,128)(2,1)} async-done(((bf16[512,1024]{1,0:T(8,128)(2,1)}), bf16[128,1024]{1,0:T(8,128)(2,1)}) %reduce-scatter.5.cloned.1.call-update) | async-done | bytes 262160 | tf_op jit(solution)/shard_map/reduce_scatter | solution.py:256
  387.4 0.0 all-gather.10.cloned.1.call-update
  387.4 0.0 all-gather.12.cloned.1.call-start
  387.5 1.6 collective-permute-start
  389.1 0.0 collective-permute-done
  389.1 0.0 copy-start.1
  389.1 0.7 copy-done.1
  389.8 0.0 all-gather.12.cloned.1.call-update
  389.8 20.1 %all-gather.10.cloned.1.call-done.left_ref = bf16[512,1024]{1,0:T(8,128)(2,1)} async-done(((bf16[128,1024]{1,0:T(8,128)(2,1)}), bf16[512,1024]{1,0:T(8,128)(2,1)}) %all-gather.10.cloned.1.call-update) | async-done | bytes 1048592 | tf_op jit(solution)/shard_map/all_gather | solution.py:266
  409.9 53.8 %all-gather.12.cloned.1.call-done = bf16[1024,1024]{1,0:T(8,128)(2,1)} async-done(((bf16[128,1024]{1,0:T(8,128)(2,1)}), bf16[1024,1024]{1,0:T(8,128)(2,1)}) %all-gather.12.cloned.1.call-update) | async-done | bytes 2097168 | tf_op jit(solution)/shard_map/all_gather | solution.py:267
  463.7 8.9 %shard_map.62 = f32[1024,2048]{1,0:T(8,128)} custom-call(bf16[512,1024]{1,0:T(8,128)(2,1)} %all-gather.10.cloned.1.call-done.left_ref, bf16[2,512,1024]{2,1,0:T(8,128)(2,1)} %bitcast.15), custom_call_target="tpu_custom_call" | custom-call | tf_op jit(solution)/shard_map/pallas_call | solution.py:193
  (1 shorter events, 0.0 us)
Async XLA Ops:
  8.0 145.8 %all-reduce.3.cloned.1.call-start = ((), (), s32[]{:S(2)}) async-start(), calls=%async_computation.2 | async-start | bytes 3670016 | tf_op jit(solution)/shard_map/psum | solution.py:226
  16.8 240.2 %all-gather.6.cloned.1.call-start = ((), (), s32[]{:S(2)}) async-start(), calls=%async_computation.3 | async-start | bytes 2359296 | tf_op jit(solution)/shard_map/all_gather | solution.py:231
  153.9 103.1 %reduce-scatter.3.cloned.1.call-start = ((), (), s32[]{:S(2)}) async-start(), calls=%async_computation.4 | async-start | bytes 4587520 | tf_op jit(solution)/shard_map/reduce_scatter | solution.py:227
  154.4 195.5 %all-reduce.5.cloned.1.call-start = ((), (), s32[]{:S(2)}) async-start(), calls=%async_computation.6 | async-start | bytes 7340032 | tf_op jit(solution)/shard_map/psum | solution.py:230
  155.2 194.8 %all-gather.8.cloned.1.call-start = ((), (), s32[]{:S(2)}) async-start(), calls=%async_computation.5 | async-start | bytes 2293760 | tf_op jit(solution)/shard_map/all_gather | solution.py:242
  155.2 1.5 copy-start
  256.9 5.9 %copy-start.2 = (s32[7]{0:T(128)S(1)}, s32[7]{0:T(128)}, u32[]{:S(2)}) copy-start(s32[7]{0:T(128)} %param.7) | copy-start | bytes 88
  262.5 124.9 %reduce-scatter.5.cloned.1.call-start = ((), (), s32[]{:S(2)}) async-start(), calls=%async_computation.7 | async-start | bytes 1310720 | tf_op jit(solution)/shard_map/reduce_scatter | solution.py:256
  262.9 97.5 %copy-start.3 = (bf16[512,2048]{1,0:T(8,128)(2,1)S(1)}, bf16[512,2048]{1,0:T(8,128)(2,1)}, u32[]{:S(2)}) copy-start(bf16[512,2048]{1,0:T(8,128)(2,1)} %all-gather.6.cloned.1.call-done) | copy-start | bytes 6291460
  358.3 2.0 copy-start.4
  363.8 46.1 %all-gather.10.cloned.1.call-start = ((), (), s32[]{:S(2)}) async-start(), calls=%async_computation.8 | async-start | bytes 1310720 | tf_op jit(solution)/shard_map/all_gather | solution.py:266
  387.4 76.3 %all-gather.12.cloned.1.call-start = ((), (), s32[]{:S(2)}) async-start(), calls=%async_computation.9 | async-start | bytes 2359296 | tf_op jit(solution)/shard_map/all_gather | solution.py:267
  387.5 1.6 collective-permute-start
  389.1 0.7 copy-start.1
Sparse Core Ops, SparseCore 0:
  16.9 136.9 all-reduce.2
  156.0 48.0 all-gather.5
  208.4 141.5 all-reduce.4
Sparse Core Ops, SparseCore 1:
  157.4 40.0 reduce-scatter.2
  262.6 19.8 all-gather.7
  363.8 23.5 reduce-scatter.4
  389.0 20.8 all-gather.9
  412.6 51.1 all-gather.11

commit v3 on v2

--- a/solution.py
+++ b/solution.py
@@ -223,11 +223,13 @@
         ]
     ).astype(jnp.int32)
     columns, own_low = pick_columns(places, inverse_factor)
-    low = lax.psum(own_low, ("rows", "mp"))
+    own_kept = pick_rows(places, weight)
+    share = lax.psum_scatter(own_low, "mp", scatter_dimension=0, tiled=True)
+    share = lax.psum(share, "rows")
+    share, own_kept, calib, columns = lax.optimization_barrier((share, own_kept, calib, columns))
+    low = lax.all_gather(share, "mp", axis=0, tiled=True)
+    kept_rows = lax.psum(own_kept, "rows")
     own_columns = lax.psum_scatter(columns, "mp", scatter_dimension=0, tiled=True)
-    own_kept = pick_rows(places, weight)
-    low, own_kept, calib = lax.optimization_barrier((low, own_kept, calib))
-    kept_rows = lax.psum(own_kept, "rows")
     all_calib = lax.all_gather(calib, "rows", axis=0, tiled=True)
 
     negative = minus_inverse(low, block_count * BLOCK)
@@ -263,6 +265,7 @@
             target = ((r % per_col) * mp_parts + m) * mp_parts + r // per_col
             pairs.append((r * mp_parts + m, target))
     moved = lax.ppermute(own_rows, ("rows", "mp"), pairs)
+    own_rows, moved = lax.optimization_barrier((own_rows, moved))
     left = lax.all_gather(own_rows, "mp", axis=0, tiled=True)
     right = lax.all_gather(moved, "rows", axis=0, tiled=False)
     right = right.reshape(per_col, token_count, rows_dev)

time: 481 us -> 555 us (1.15)
  waiting for transfers between devices: 317 us -> 393 us
    psum x1, waiting for transfers between devices: 131 us -> 70 us  [shards(): share = lax.psum(share, 'rows')]
    psum x1, waiting for transfers between devices: 87.1 us -> 133 us  [shards(): kept_rows = lax.psum(own_kept, 'rows')]
    reduce_scatter x0 -> x1, waiting for transfers between devices: none -> 32.5 us  [shards(): share = lax.psum_scatter(own_low, 'mp', scatter_dimension=0, tiled=True)]
    all_gather x1, waiting for transfers between devices: 0.01 us -> 22.1 us  [shards(): lax.all_gather(own_factors.astype(jnp.bfloat16), 'mp', axis=0, tiled=True)]
    all_gather x0 -> x1, waiting for transfers between devices: none -> 20.2 us  [shards(): low = lax.all_gather(share, 'mp', axis=0, tiled=True)]
    all_gather x1, waiting for transfers between devices: 20.1 us -> 36.5 us  [shards(): left = lax.all_gather(own_rows, 'mp', axis=0, tiled=True)]
  transfers between devices with their start and end apart: 9 -> 11, of which waited for: 5 -> 8; matrix products, arithmetic and copies ran while one was open for 1% -> 1% of each run, Pallas kernels for 22% -> 19%
where the time goes in v3:
time: 555 us
  waiting for transfers between devices  393 us (71%)
  Pallas kernels  122 us (22%)
  matrix products  17.2 us (3%)
  between operations  14.2 us (3%)
    psum x1, waiting for transfers between devices, shards(): kept_rows = lax.psum(own_kept, 'rows')  133 us
    pallas_call x1, Pallas kernels, minus_inverse(): pl.pallas_call(invert_kernel, out_shape=jax.ShapeDtypeStruct((order, orde...  100 us
    psum x1, waiting for transfers between devices, shards(): share = lax.psum(share, 'rows')  70 us
    all_gather x1, waiting for transfers between devices, shards(): right = lax.all_gather(moved, 'rows', axis=0, tiled=False)  51.7 us
    all_gather x1, waiting for transfers between devices, shards(): left = lax.all_gather(own_rows, 'mp', axis=0, tiled=True)  36.5 us
    reduce_scatter x1, waiting for transfers between devices, shards(): share = lax.psum_scatter(own_low, 'mp', scatter_dimension=0, tiled=True)  32.5 us
    reduce_scatter x1, waiting for transfers between devices, shards(): lax.psum_scatter((partial_value * out_scale).astype(jnp.bfloat16), 'mp',...  24.9 us
    all_gather x1, waiting for transfers between devices, shards(): lax.all_gather(own_factors.astype(jnp.bfloat16), 'mp', axis=0, tiled=True)  22.1 us
  transfers between devices with their start and end apart: 11, of which 8 were waited for; matrix products, arithmetic and copies ran while one was open for 1% of the time, Pallas kernels for 19%

profile of v3, /device:TPU:0, one launch (start us, length us, event | category | flops | bytes accessed | tf_op | source)
XLA Modules:
  0.0 554.7 jit_solution(10727508827463043611)
XLA Ops:
  7.2 0.0 reduce-scatter.4.cloned.1.call-start
  7.2 0.7 fusion.4
  7.9 0.7 fusion.7
  8.5 0.6 pad_add_fusion.places_ref
  9.1 7.2 %shard_map.59 = (f32[1024,896]{1,0:T(8,128)}, f32[128,3584]{1,0:T(8,128)}) custom-call(s32[4,7]{1,0:T(4,128)} %pad_add_fusion.places_ref, f32[1024,2048]{1,0:T(8,128)} %factor_ref.1), custom_call_target="tpu_custom_call" | custom-call | tf_op jit(solution)/shard_map/pallas_call | solution.py:141
  16.3 0.0 reduce-scatter.4.cloned.1.call-update
  16.4 0.0 all-reduce.3.cloned.1.call-start
  16.4 32.5 %reduce-scatter.4.cloned.1.call-done = f32[32,3584]{1,0:T(8,128)} async-done(((f32[128,3584]{1,0:T(8,128)}), f32[32,3584]{1,0:T(8,128)}) %reduce-scatter.4.cloned.1.call-update) | async-done | bytes 458768 | tf_op jit(solution)/shard_map/reduce_scatter | solution.py:227
  48.9 0.0 all-reduce.3.cloned.1.call-update
  48.9 0.0 all-gather.7.cloned.1.call-start
  49.0 5.8 %shard_map.60 = bf16[896,2048]{1,0:T(8,128)(2,1)} custom-call(s32[4,7]{1,0:T(4,128)} %pad_add_fusion.places_ref, bf16[1024,2048]{1,0:T(8,128)(2,1)} %weight_ref.1), custom_call_target="tpu_custom_call" | custom-call | tf_op jit(solution)/shard_map/pallas_call | solution.py:168
  54.8 70.0 %all-reduce.3.cloned.1.call-done = f32[32,3584]{1,0:T(8,128)} async-done(((f32[32,3584]{1,0:T(8,128)}), f32[32,3584]{1,0:T(8,128)}) %all-reduce.3.cloned.1.call-update) | async-done | bytes 458768 | tf_op jit(solution)/shard_map/psum | solution.py:228
  124.7 0.0 all-gather.7.cloned.1.call-update
  124.7 0.0 all-gather.9.cloned.1.call-start
  124.8 0.5 all-gather.9.cloned.1.call-update
  125.3 0.0 reduce-scatter.6.cloned.1.call-start
  125.4 0.5 reduce-scatter.6.cloned.1.call-update
  125.9 0.0 all-reduce.5.cloned.1.call-start
  126.0 0.5 all-reduce.5.cloned.1.call-update
  126.5 0.0 all-gather.11.cloned.1.call-start
  126.5 20.2 %all-gather.7.cloned.1.call-done.low_ref = f32[128,3584]{1,0:T(8,128)} async-done(((f32[32,3584]{1,0:T(8,128)}), f32[128,3584]{1,0:T(8,128)}) %all-gather.7.cloned.1.call-update) | async-done | bytes 1835024 | tf_op jit(solution)/shard_map/all_gather | solution.py:230
  146.7 1.5 copy-done
  148.2 100.1 %shard_map.61 = f32[896,896]{1,0:T(8,128)S(1)} custom-call(f32[128,3584]{1,0:T(8,128)S(1)} %copy-done), custom_call_target="tpu_custom_call" | custom-call | flops 60000002048 | bytes 6422528 | tf_op jit(solution)/shard_map/pallas_call | solution.py:108
  248.4 0.0 copy-start.2
  248.4 0.0 all-gather.9.cloned.1.call-done
  248.4 0.0 reduce-scatter.6.cloned.1.call-done
  248.4 5.5 fusion
  253.9 0.0 all-gather.11.cloned.1.call-update
  254.0 0.2 reduce-scatter.8.cloned.1.call-start
  254.2 0.1 compare_reduce_fusion
  254.3 133.3 %all-reduce.5.cloned.1.call-done = bf16[896,2048]{1,0:T(8,128)(2,1)} async-done(((bf16[896,2048]{1,0:T(8,128)(2,1)}), bf16[896,2048]{1,0:T(8,128)(2,1)}) %all-reduce.5.cloned.1.call-update) | async-done | bytes 3670032 | tf_op jit(solution)/shard_map/psum | solution.py:231
  387.7 22.1 %all-gather.11.cloned.1.call-done = bf16[1024,896]{1,0:T(8,128)(2,1)} async-done(((bf16[256,896]{1,0:T(8,128)(2,1)}), bf16[1024,896]{1,0:T(8,128)(2,1)}) %all-gather.11.cloned.1.call-update) | async-done | bytes 1835024 | tf_op jit(solution)/shard_map/all_gather | solution.py:244
  409.7 8.3 %select_convert_fusion = bf16[1024,2048]{1,0:T(8,128)(2,1)S(1)} fusion(bf16[1024,2048]{1,0:T(8,128)(2,1)} %weight_ref.1, pred[1024]{0:T(1024)(128)(4,1)S(1)} %compare_reduce_fusion, bf16[1024,896]{1,0:T(8,128)(2,1)} %all-gather.11.cloned.1.call-done, bf16[896,2048]{1,0:T(8,128)(2,1)} %all-reduce.5.cloned.1.call-done), kind=kOutput, calls=%fused_computation | convolution fusion | flops 3766484992 | bytes 13894656 | tf_op jit(solution)/shard_map/dot_general | solution.py:245
  418.1 0.0 copy-start.4
  418.1 2.0 copy-done.4
  420.1 3.4 multiply_convert_fusion
  423.5 0.0 reduce-scatter.8.cloned.1.call-update
  423.5 0.0 all-gather.13.cloned.1.call-start
  423.6 24.9 %reduce-scatter.8.cloned.1.call-done = bf16[128,1024]{1,0:T(8,128)(2,1)} async-done(((bf16[512,1024]{1,0:T(8,128)(2,1)}), bf16[128,1024]{1,0:T(8,128)(2,1)}) %reduce-scatter.8.cloned.1.call-update) | async-done | bytes 262160 | tf_op jit(solution)/shard_map/reduce_scatter | solution.py:258
  448.5 1.6 collective-permute-start
  450.1 0.0 collective-permute-done
  450.1 0.0 all-gather.13.cloned.1.call-update
  450.1 0.0 all-gather.15.cloned.1.call-start
  450.2 0.6 copy-done.1
  450.8 0.0 all-gather.15.cloned.1.call-update
  450.8 36.5 %all-gather.13.cloned.1.call-done.left_ref = bf16[512,1024]{1,0:T(8,128)(2,1)} async-done(((bf16[128,1024]{1,0:T(8,128)(2,1)}), bf16[512,1024]{1,0:T(8,128)(2,1)}) %all-gather.13.cloned.1.call-update) | async-done | bytes 1048592 | tf_op jit(solution)/shard_map/all_gather | solution.py:269
  487.3 51.7 %all-gather.15.cloned.1.call-done = bf16[1024,1024]{1,0:T(8,128)(2,1)} async-done(((bf16[128,1024]{1,0:T(8,128)(2,1)}), bf16[1024,1024]{1,0:T(8,128)(2,1)}) %all-gather.15.cloned.1.call-update) | async-done | bytes 2097168 | tf_op jit(solution)/shard_map/all_gather | solution.py:270
  539.0 8.9 %shard_map.62 = f32[1024,2048]{1,0:T(8,128)} custom-call(bf16[512,1024]{1,0:T(8,128)(2,1)} %all-gather.13.cloned.1.call-done.left_ref, bf16[2,512,1024]{2,1,0:T(8,128)(2,1)} %bitcast.15), custom_call_target="tpu_custom_call" | custom-call | tf_op jit(solution)/shard_map/pallas_call | solution.py:193
  (6 shorter events, 0.0 us)
Async XLA Ops:
  7.2 41.7 %reduce-scatter.4.cloned.1.call-start = ((), (), s32[]{:S(2)}) async-start(), calls=%async_computation.3 | async-start | bytes 2293760 | tf_op jit(solution)/shard_map/reduce_scatter | solution.py:227
  16.4 108.4 %all-reduce.3.cloned.1.call-start = ((), (), s32[]{:S(2)}) async-start(), calls=%async_computation.4 | async-start | bytes 917504 | tf_op jit(solution)/shard_map/psum | solution.py:228
  48.9 97.8 %all-gather.7.cloned.1.call-start = ((), (), s32[]{:S(2)}) async-start(), calls=%async_computation.5 | async-start | bytes 2293760 | tf_op jit(solution)/shard_map/all_gather | solution.py:230
  124.7 123.6 %all-gather.9.cloned.1.call-start = ((), (), s32[]{:S(2)}) async-start(), calls=%async_computation.6 | async-start | bytes 2359296 | tf_op jit(solution)/shard_map/all_gather | solution.py:233
  125.3 123.1 %reduce-scatter.6.cloned.1.call-start = ((), (), s32[]{:S(2)}) async-start(), calls=%async_computation.7 | async-start | bytes 4587520 | tf_op jit(solution)/shard_map/reduce_scatter | solution.py:232
  125.9 261.8 %all-reduce.5.cloned.1.call-start = ((), (), s32[]{:S(2)}) async-start(), calls=%async_computation.9 | async-start | bytes 7340032 | tf_op jit(solution)/shard_map/psum | solution.py:231
  126.5 283.3 %all-gather.11.cloned.1.call-start = ((), (), s32[]{:S(2)}) async-start(), calls=%async_computation.8 | async-start | bytes 2293760 | tf_op jit(solution)/shard_map/all_gather | solution.py:244
  146.7 1.5 copy-start
  248.4 5.9 %copy-start.2 = (s32[7]{0:T(128)S(1)}, s32[7]{0:T(128)}, u32[]{:S(2)}) copy-start(s32[7]{0:T(128)} %param.7) | copy-start | bytes 88
  254.0 194.5 %reduce-scatter.8.cloned.1.call-start = ((), (), s32[]{:S(2)}) async-start(), calls=%async_computation.10 | async-start | bytes 1310720 | tf_op jit(solution)/shard_map/reduce_scatter | solution.py:258
  254.3 165.8 %copy-start.3 = (bf16[512,2048]{1,0:T(8,128)(2,1)S(1)}, bf16[512,2048]{1,0:T(8,128)(2,1)}, u32[]{:S(2)}) copy-start(bf16[512,2048]{1,0:T(8,128)(2,1)} %all-gather.9.cloned.1.call-done) | copy-start | bytes 6291460
  418.1 2.0 copy-start.4
  423.5 63.8 %all-gather.13.cloned.1.call-start = ((), (), s32[]{:S(2)}) async-start(), calls=%async_computation.11 | async-start | bytes 1310720 | tf_op jit(solution)/shard_map/all_gather | solution.py:269
  448.5 1.6 collective-permute-start
  450.1 0.7 copy-start.1
  450.1 88.8 %all-gather.15.cloned.1.call-start = ((), (), s32[]{:S(2)}) async-start(), calls=%async_computation.12 | async-start | bytes 2359296 | tf_op jit(solution)/shard_map/all_gather | solution.py:270
Sparse Core Ops, SparseCore 0:
  16.5 32.3 reduce-scatter.3
  52.3 72.3 all-reduce.2
  126.3 20.3 all-gather.6
  148.7 49.2 all-gather.8
  200.9 39.6 reduce-scatter.5
  244.8 142.8 all-reduce.4
  389.8 19.9 all-gather.10
  423.6 24.8 reduce-scatter.7
  450.2 37.0 all-gather.12
  489.8 49.0 all-gather.14

commit v4 on v2

--- a/solution.py
+++ b/solution.py
@@ -9,6 +9,7 @@
 
 BLOCK = 128
 SUB = 8
+GROUP = 4
 
 
 def split3(value):
@@ -23,32 +24,44 @@
     lane = lax.broadcasted_iota(jnp.int32, (SUB, BLOCK), 1)
     sublane = lax.broadcasted_iota(jnp.int32, (SUB, BLOCK), 0)
     wide = (SUB, BLOCK)
-    for p in range(0, BLOCK, 2):
-        q = p + 1
+    for p in range(0, BLOCK, GROUP):
         own, s = p // SUB, p % SUB
-        row_p = jnp.broadcast_to(tiles[own][s : s + 1, :], wide)
-        row_q = jnp.broadcast_to(tiles[own][s + 1 : s + 2, :], wide)
-        d_p = jnp.broadcast_to(row_p[:, p : p + 1], wide)
-        off = jnp.broadcast_to(row_p[:, q : q + 1], wide)
-        d_q = jnp.broadcast_to(row_q[:, q : q + 1], wide)
-        inv_p = 1.0 / d_p
-        ratio = off * inv_p
-        m_qq = 1.0 / (d_q - off * ratio)
-        m_pq = -ratio * m_qq
-        m_pp = inv_p - ratio * m_pq
-        is_p, is_q = lane == p, lane == q
-        u_p = m_pp * row_p + m_pq * row_q
-        u_q = m_pq * row_p + m_qq * row_q
-        u_p = jnp.where(is_p, -m_pp, jnp.where(is_q, -m_pq, u_p))
-        u_q = jnp.where(is_p, -m_pq, jnp.where(is_q, -m_qq, u_q))
-        pivot = is_p | is_q
+        rows = [
+            jnp.broadcast_to(tiles[own][s + a : s + a + 1, :], wide) for a in range(GROUP)
+        ]
+        small = {}
+        for a in range(GROUP):
+            for b in range(a, GROUP):
+                small[a, b] = jnp.broadcast_to(rows[a][:, p + b : p + b + 1], wide)
+        for k in range(GROUP):
+            inv = 1.0 / small[k, k]
+            old = {a: small[min(a, k), max(a, k)] for a in range(GROUP) if a != k}
+            scaled = {a: value * inv for a, value in old.items()}
+            for a in old:
+                for b in old:
+                    if a <= b:
+                        small[a, b] = small[a, b] - old[a] * scaled[b]
+                small[min(a, k), max(a, k)] = scaled[a]
+            small[k, k] = -inv
+        pivots = [lane == p + a for a in range(GROUP)]
+        updates = []
+        for a in range(GROUP):
+            update = -small[0, a] * rows[0]
+            for b in range(1, GROUP):
+                update = update - small[min(a, b), max(a, b)] * rows[b]
+            for b in range(GROUP):
+                update = jnp.where(pivots[b], small[min(a, b), max(a, b)], update)
+            updates.append(update)
+        inside = (lane >= p) & (lane < p + GROUP)
         new = []
         for t in range(len(tiles)):
-            col_p = jnp.broadcast_to(tiles[t][:, p : p + 1], wide)
-            col_q = jnp.broadcast_to(tiles[t][:, q : q + 1], wide)
-            value = jnp.where(pivot, 0.0, tiles[t]) - col_p * u_p - col_q * u_q
+            value = jnp.where(inside, 0.0, tiles[t])
+            for a in range(GROUP):
+                column = jnp.broadcast_to(tiles[t][:, p + a : p + a + 1], wide)
+                value = value - column * updates[a]
             if t == own:
-                value = jnp.where(sublane == s, u_p, jnp.where(sublane == s + 1, u_q, value))
+                for a in range(GROUP):
+                    value = jnp.where(sublane == s + a, updates[a], value)
             new.append(value)
         tiles = new
     return tiles
@@ -225,10 +238,9 @@
     columns, own_low = pick_columns(places, inverse_factor)
     low = lax.psum(own_low, ("rows", "mp"))
     own_columns = lax.psum_scatter(columns, "mp", scatter_dimension=0, tiled=True)
-    own_kept = pick_rows(places, weight)
-    low, own_kept, calib = lax.optimization_barrier((low, own_kept, calib))
+    all_calib = lax.all_gather(calib, "rows", axis=0, tiled=True)
+    low, own_kept = lax.optimization_barrier((low, pick_rows(places, weight)))
     kept_rows = lax.psum(own_kept, "rows")
-    all_calib = lax.all_gather(calib, "rows", axis=0, tiled=True)
 
     negative = minus_inverse(low, block_count * BLOCK)
     negative, all_calib, own_columns = lax.optimization_barrier((negative, all_calib, own_columns))

time: 481 us -> 438 us (0.911)
  Pallas kernels: 122 us -> 84.1 us
  waiting for transfers between devices: 317 us -> 311 us
    pallas_call x1, Pallas kernels: 100 us -> 62.7 us  [minus_inverse(): pl.pallas_call(invert_kernel, out_shape=jax.ShapeDtypeStruct((order, orde...]
    psum x1, waiting for transfers between devices: 87.1 us -> 71.2 us  [shards(): kept_rows = lax.psum(own_kept, 'rows')]
    psum x1, waiting for transfers between devices: 131 us -> 141 us  [shards(): low = lax.psum(own_low, ('rows', 'mp'))]
  transfers between devices with their start and end apart: 9 -> 9, of which waited for: 5 -> 5; matrix products, arithmetic and copies ran while one was open for 1% -> 1% of each run, Pallas kernels for 22% -> 16%
where the time goes in v4:
time: 438 us; the launch traced here: 437 us
  waiting for transfers between devices  311 us (71%)
  Pallas kernels  84.1 us (19%)
  matrix products  17.2 us (4%)
  between operations  15.6 us (4%)
    psum x1, waiting for transfers between devices, shards(): low = lax.psum(own_low, ('rows', 'mp'))  141 us
    psum x1, waiting for transfers between devices, shards(): kept_rows = lax.psum(own_kept, 'rows')  71.2 us
    pallas_call x1, Pallas kernels, minus_inverse(): pl.pallas_call(invert_kernel, out_shape=jax.ShapeDtypeStruct((order, orde...  62.7 us
    all_gather x1, waiting for transfers between devices, shards(): right = lax.all_gather(moved, 'rows', axis=0, tiled=False)  53.9 us
    reduce_scatter x1, waiting for transfers between devices, shards(): lax.psum_scatter((partial_value * out_scale).astype(jnp.bfloat16), 'mp',...  23.9 us
    all_gather x1, waiting for transfers between devices, shards(): left = lax.all_gather(own_rows, 'mp', axis=0, tiled=True)  20.1 us
    pallas_call x1, Pallas kernels, gram_of(): pl.pallas_call(functools.partial(gram_kernel, token_count), grid=(parts,...  8.93 us
  transfers between devices with their start and end apart: 9, of which 5 were waited for; matrix products, arithmetic and copies ran while one was open for 1% of the time, Pallas kernels for 16%

profile of v4, /device:TPU:0, one launch (start us, length us, event | category | flops | bytes accessed | tf_op | source)
XLA Modules:
  0.0 436.5 jit_solution(15148825526252918606)
XLA Ops:
  8.0 0.0 all-reduce.3.cloned.1.call-start
  8.0 0.7 fusion.4
  8.7 0.7 fusion.7
  9.4 0.6 pad_add_fusion.places_ref
  10.0 6.6 %shard_map.59 = (f32[1024,896]{1,0:T(8,128)}, f32[128,3584]{1,0:T(8,128)}) custom-call(s32[4,7]{1,0:T(4,128)} %pad_add_fusion.places_ref, f32[1024,2048]{1,0:T(8,128)} %factor_ref.1), custom_call_target="tpu_custom_call" | custom-call | tf_op jit(solution)/shard_map/pallas_call | solution.py:154
  16.6 0.0 all-reduce.3.cloned.1.call-update
  16.6 0.0 all-gather.6.cloned.1.call-start
  16.7 0.5 all-gather.6.cloned.1.call-update
  17.2 0.0 reduce-scatter.3.cloned.1.call-start
  17.2 0.7 reduce-scatter.3.cloned.1.call-update
  17.9 0.0 all-reduce.5.cloned.1.call-start
  18.0 5.8 %shard_map.60 = bf16[896,2048]{1,0:T(8,128)(2,1)} custom-call(s32[4,7]{1,0:T(4,128)} %pad_add_fusion.places_ref, bf16[1024,2048]{1,0:T(8,128)(2,1)} %weight_ref.1), custom_call_target="tpu_custom_call" | custom-call | tf_op jit(solution)/shard_map/pallas_call | solution.py:181
  23.8 140.8 %all-reduce.3.cloned.1.call-done.low_ref = f32[128,3584]{1,0:T(8,128)} async-done(((f32[128,3584]{1,0:T(8,128)}), f32[128,3584]{1,0:T(8,128)}) %all-reduce.3.cloned.1.call-update) | async-done | bytes 1835024 | tf_op jit(solution)/shard_map/psum | solution.py:239
  164.6 0.0 all-reduce.5.cloned.1.call-update
  164.6 0.0 all-gather.8.cloned.1.call-start
  164.6 0.0 copy-start
  164.7 1.5 copy-done
  166.1 62.7 %shard_map.61 = f32[896,896]{1,0:T(8,128)S(1)} custom-call(f32[128,3584]{1,0:T(8,128)S(1)} %copy-done), custom_call_target="tpu_custom_call" | custom-call | flops 60000002048 | bytes 6422528 | tf_op jit(solution)/shard_map/pallas_call | solution.py:121
  228.9 0.0 copy-start.2
  228.9 0.0 all-gather.6.cloned.1.call-done
  228.9 0.0 reduce-scatter.3.cloned.1.call-done
  229.0 5.5 %fusion = bf16[256,896]{1,0:T(8,128)(2,1)} fusion(f32[256,896]{1,0:T(8,128)} %reduce-scatter.3.cloned.1.call-done, f32[896,896]{1,0:T(8,128)S(1)} %shard_map.61), kind=kOutput, calls=%fused_computation.3 | convolution fusion | flops 2466709504 | bytes 4587520 | tf_op jit(solution)/shard_map/dot_general | solution.py:247
  234.5 0.0 all-gather.8.cloned.1.call-update
  234.5 0.2 reduce-scatter.5.cloned.1.call-start
  234.8 0.0 copy-done.2
  234.8 0.1 compare_reduce_fusion
  234.9 0.0 copy-start.3
  234.9 71.2 %all-reduce.5.cloned.1.call-done = bf16[896,2048]{1,0:T(8,128)(2,1)} async-done(((bf16[896,2048]{1,0:T(8,128)(2,1)}), bf16[896,2048]{1,0:T(8,128)(2,1)}) %all-reduce.5.cloned.1.call-update) | async-done | bytes 3670032 | tf_op jit(solution)/shard_map/psum | solution.py:243
  306.0 0.0 all-gather.8.cloned.1.call-done
  306.0 8.4 %select_convert_fusion = bf16[1024,2048]{1,0:T(8,128)(2,1)S(1)} fusion(bf16[1024,2048]{1,0:T(8,128)(2,1)} %weight_ref.1, pred[1024]{0:T(1024)(128)(4,1)S(1)} %compare_reduce_fusion, bf16[1024,896]{1,0:T(8,128)(2,1)} %all-gather.8.cloned.1.call-done, bf16[896,2048]{1,0:T(8,128)(2,1)} %all-reduce.5.cloned.1.call-done), kind=kOutput, calls=%fused_computation | convolution fusion | flops 3766484992 | bytes 13894656 | tf_op jit(solution)/shard_map/dot_general | solution.py:255
  314.4 0.0 copy-start.4
  314.4 2.0 copy-done.4
  316.4 0.0 copy-done.3
  316.4 3.4 multiply_convert_fusion
  319.8 0.0 reduce-scatter.5.cloned.1.call-update
  319.8 0.0 all-gather.10.cloned.1.call-start
  319.9 23.9 %reduce-scatter.5.cloned.1.call-done = bf16[128,1024]{1,0:T(8,128)(2,1)} async-done(((bf16[512,1024]{1,0:T(8,128)(2,1)}), bf16[128,1024]{1,0:T(8,128)(2,1)}) %reduce-scatter.5.cloned.1.call-update) | async-done | bytes 262160 | tf_op jit(solution)/shard_map/reduce_scatter | solution.py:268
  343.8 0.0 all-gather.10.cloned.1.call-update
  343.8 0.0 all-gather.12.cloned.1.call-start
  343.9 1.6 collective-permute-start
  345.5 0.0 collective-permute-done
  345.5 0.0 copy-start.1
  345.5 0.7 copy-done.1
  346.2 0.0 all-gather.12.cloned.1.call-update
  346.2 20.1 %all-gather.10.cloned.1.call-done.left_ref = bf16[512,1024]{1,0:T(8,128)(2,1)} async-done(((bf16[128,1024]{1,0:T(8,128)(2,1)}), bf16[512,1024]{1,0:T(8,128)(2,1)}) %all-gather.10.cloned.1.call-update) | async-done | bytes 1048592 | tf_op jit(solution)/shard_map/all_gather | solution.py:278
  366.3 53.9 %all-gather.12.cloned.1.call-done = bf16[1024,1024]{1,0:T(8,128)(2,1)} async-done(((bf16[128,1024]{1,0:T(8,128)(2,1)}), bf16[1024,1024]{1,0:T(8,128)(2,1)}) %all-gather.12.cloned.1.call-update) | async-done | bytes 2097168 | tf_op jit(solution)/shard_map/all_gather | solution.py:279
  420.1 8.9 %shard_map.62 = f32[1024,2048]{1,0:T(8,128)} custom-call(bf16[512,1024]{1,0:T(8,128)(2,1)} %all-gather.10.cloned.1.call-done.left_ref, bf16[2,512,1024]{2,1,0:T(8,128)(2,1)} %bitcast.15), custom_call_target="tpu_custom_call" | custom-call | tf_op jit(solution)/shard_map/pallas_call | solution.py:206
  (1 shorter events, 0.0 us)
Async XLA Ops:
  8.0 156.6 %all-reduce.3.cloned.1.call-start = ((), (), s32[]{:S(2)}) async-start(), calls=%async_computation.2 | async-start | bytes 3670016 | tf_op jit(solution)/shard_map/psum | solution.py:239
  16.6 212.3 %all-gather.6.cloned.1.call-start = ((), (), s32[]{:S(2)}) async-start(), calls=%async_computation.3 | async-start | bytes 2359296 | tf_op jit(solution)/shard_map/all_gather | solution.py:241
  17.2 211.8 %reduce-scatter.3.cloned.1.call-start = ((), (), s32[]{:S(2)}) async-start(), calls=%async_computation.4 | async-start | bytes 4587520 | tf_op jit(solution)/shard_map/reduce_scatter | solution.py:240
  17.9 288.1 %all-reduce.5.cloned.1.call-start = ((), (), s32[]{:S(2)}) async-start(), calls=%async_computation.6 | async-start | bytes 7340032 | tf_op jit(solution)/shard_map/psum | solution.py:243
  164.6 141.4 %all-gather.8.cloned.1.call-start = ((), (), s32[]{:S(2)}) async-start(), calls=%async_computation.5 | async-start | bytes 2293760 | tf_op jit(solution)/shard_map/all_gather | solution.py:254
  164.6 1.5 copy-start
  228.9 5.9 %copy-start.2 = (s32[7]{0:T(128)S(1)}, s32[7]{0:T(128)}, u32[]{:S(2)}) copy-start(s32[7]{0:T(128)} %param.7) | copy-start | bytes 88
  234.5 109.3 %reduce-scatter.5.cloned.1.call-start = ((), (), s32[]{:S(2)}) async-start(), calls=%async_computation.7 | async-start | bytes 1310720 | tf_op jit(solution)/shard_map/reduce_scatter | solution.py:268
  234.9 81.5 %copy-start.3 = (bf16[512,2048]{1,0:T(8,128)(2,1)S(1)}, bf16[512,2048]{1,0:T(8,128)(2,1)}, u32[]{:S(2)}) copy-start(bf16[512,2048]{1,0:T(8,128)(2,1)} %all-gather.6.cloned.1.call-done) | copy-start | bytes 6291460
  314.4 2.0 copy-start.4
  319.8 46.5 %all-gather.10.cloned.1.call-start = ((), (), s32[]{:S(2)}) async-start(), calls=%async_computation.8 | async-start | bytes 1310720 | tf_op jit(solution)/shard_map/all_gather | solution.py:278
  343.8 76.3 %all-gather.12.cloned.1.call-start = ((), (), s32[]{:S(2)}) async-start(), calls=%async_computation.9 | async-start | bytes 2359296 | tf_op jit(solution)/shard_map/all_gather | solution.py:279
  343.9 1.6 collective-permute-start
  345.5 0.7 copy-start.1
Sparse Core Ops, SparseCore 0:
  16.7 147.7 all-reduce.2
  167.7 40.1 reduce-scatter.2
  234.6 20.0 all-gather.7
  319.9 23.8 reduce-scatter.4
  345.2 21.0 all-gather.9
  368.8 51.2 all-gather.11
Sparse Core Ops, SparseCore 1:
  19.2 54.3 all-gather.5
  164.7 141.3 all-reduce.4
